TPU v7x, 256 devices: a whole 4x4x8 slice. The times are simulated.
256 devices in a mesh: leaf: 32 (over x, y, core), front: 8 (over z).
Axes of the slice: x: 4, y: 4, z: 8, core: 2. Of those that a mesh axis runs over, the one named last changes fastest.
Arguments:
- child_updates: float32 [32768, 1024], P('leaf', 'front'), as said below
- initial_one: float32 [32768, 2048], P('leaf', 'front'), as said below
- initial_two: float32 [16384, 2048], P('leaf', 'front'), as said below
- pattern_one: int32 [16, 16, 16], replicated, may hold values 0 or 1
- pattern_two: int32 [8, 16, 16], replicated, may hold values 0 or 1
- parent_map_one: int32 [16, 2, 16], replicated, may hold values from 0 to 15, each once within a row
- parent_map_two: int32 [8, 2, 16], replicated, may hold values from 0 to 15, each once within a row
Outputs:
- factor_one: float32 [32768, 1024], P('leaf', 'front')
- factor_two: float32 [16384, 1024], P('leaf', 'front')
- schur_two: float32 [8192, 1024], P('leaf', 'front')
Inputs may be any that keep to these rules, and one draw needn't show every extreme that they name: `parent_map_one`: each row is a permutation of 0 to 15; only its first 8 entries are used. `parent_map_two`: each row is a permutation of 0 to 15; only its first 8 entries are used. `initial_one`: each 2048 x 2048 front block is symmetric, and positive definite after any symmetric block mask. `initial_two`: each 2048 x 2048 front block is symmetric, and positive definite after any symmetric block mask. `child_updates`: each 1024 x 1024 matrix is symmetric positive definite.
All inputs are finite; a program needn't handle non-finite values.
Results may differ from a plain program's by a relative error of at most 0.0003.
Values sent between devices are 32-bit elements; how exact they have to be, the bound alone decides.
No kernel may reach another device: no remote copies, remote signals or barrier semaphores. Data moves between devices by JAX's collectives and lax.ppermute only.
A program may use at most 128 MiB of HBM per device.

v0:
```python
import jax
import jax.numpy as jnp
from jax import lax
from jax.sharding import PartitionSpec as P

BLK = 128
SEP = 1024
UPD = 1024
FR = 2048
HIGHEST = lax.Precision.HIGHEST


def swapped(block, axis, stride):
    count = lax.axis_size(axis)
    route = []
    for low in range(count):
        high = low | 1 << stride
        if high != low and high < count:
            route += [(low, high), (high, low)]
    return lax.ppermute(block, axis, route)


def spread(block, axis, holder):
    block = jnp.where(lax.axis_index(axis) == holder, block, jnp.zeros_like(block))
    return lax.psum(block, axis)


def solve_rows(chol_block, right_side):
    return jax.scipy.linalg.solve_triangular(chol_block, right_side.T, lower=True).T


def gather_subcube(pieces, level_depth, leaf_index):
    for bit_number in range(level_depth):
        partner = swapped(pieces, "leaf", bit_number)
        upper_half = leaf_index >> bit_number & 1 == 1
        pieces = jnp.where(
            upper_half, jnp.concatenate([partner, pieces], 0), jnp.concatenate([pieces, partner], 0)
        )
    return pieces


def fetch_rows(pieces, wanted, level_depth, leaf_index):
    columns = pieces.shape[1]
    full_panel = gather_subcube(pieces, level_depth, leaf_index)
    return jnp.take(full_panel.reshape(FR // BLK, BLK, columns), wanted, axis=0).reshape(
        wanted.shape[0] * BLK, columns
    )


def merge_halves(placed, level_depth, leaf_index):
    for bit_number in reversed(range(level_depth)):
        middle = placed.shape[0] // 2
        upper_half = leaf_index >> bit_number & 1 == 1
        kept_half = jnp.where(upper_half, placed[middle:], placed[:middle])
        given_half = jnp.where(upper_half, placed[:middle], placed[middle:])
        placed = kept_half + swapped(given_half, "leaf", bit_number)
    return placed


def assemble(
    child_tile, initial, pattern, parent_map, level_depth, leaf_index, front_index, col_blocks
):
    group_share = 2**level_depth
    child_share = group_share // 2
    front_group = leaf_index // group_share
    child_side = leaf_index // child_share % 2
    child_sub = leaf_index % child_share
    sub_index = leaf_index % group_share
    update_blocks = UPD // BLK
    front_blocks = FR // BLK
    tile_cols = 2 * col_blocks * BLK
    gathered = lax.all_gather(child_tile, "front", axis=1, tiled=True)
    child_rows = gathered.shape[0]
    child_row_blocks = child_rows // BLK
    both_maps = lax.dynamic_index_in_dim(parent_map, front_group, 0, keepdims=False)
    block_map = lax.dynamic_index_in_dim(both_maps, child_side, 0, keepdims=False)[:update_blocks]
    target_cols = 2 * col_blocks * front_index + jnp.arange(2 * col_blocks, dtype=jnp.int32)
    col_pick = (block_map[:, None] == target_cols[None, :]).astype(jnp.float32)
    picked = jnp.einsum(
        "rik,it->rtk", gathered.reshape(child_rows, update_blocks, BLK), col_pick, precision=HIGHEST
    )
    my_map = lax.dynamic_slice_in_dim(block_map, child_sub * child_row_blocks, child_row_blocks)
    row_place = (jnp.arange(front_blocks, dtype=jnp.int32)[:, None] == my_map[None, :]).astype(
        jnp.float32
    )
    placed = jnp.einsum(
        "ba,akc->bkc",
        row_place,
        picked.reshape(child_row_blocks, BLK, tile_cols),
        precision=HIGHEST,
    ).reshape(FR, tile_cols)
    merged = merge_halves(placed, level_depth, leaf_index)
    own_blocks = front_blocks // group_share
    whole_pattern = lax.dynamic_index_in_dim(pattern, front_group, 0, keepdims=False)
    row_part = lax.dynamic_slice_in_dim(whole_pattern, sub_index * own_blocks, own_blocks, 0)
    row_part = lax.dynamic_slice_in_dim(row_part, 2 * col_blocks * front_index, 2 * col_blocks, 1)
    col_part = lax.dynamic_slice_in_dim(
        whole_pattern, 2 * col_blocks * front_index, 2 * col_blocks, 0
    )
    col_part = lax.dynamic_slice_in_dim(col_part, sub_index * own_blocks, own_blocks, 1)
    row_ids = sub_index * own_blocks + jnp.arange(own_blocks, dtype=jnp.int32)
    keep_blocks = (row_part == 1) | (col_part.T == 1) | (row_ids[:, None] == target_cols[None, :])
    keep_mask = (
        jnp.broadcast_to(keep_blocks[:, None, :, None], (own_blocks, BLK, 2 * col_blocks, BLK))
        .reshape(own_blocks * BLK, tile_cols)
        .astype(jnp.float32)
    )
    return (initial * keep_mask + merged, row_ids, target_cols)


def factor_panels(
    front_tile, row_ids, target_cols, level_depth, leaf_index, front_index, col_blocks
):
    tile_rows = front_tile.shape[0]
    panel_width = col_blocks * BLK
    row_odd = jnp.repeat(row_ids % 2 == 1, BLK)
    row_sep = jnp.repeat(row_ids // 2, BLK)
    col_odd = jnp.repeat(target_cols % 2 == 1, BLK)
    col_sep = jnp.repeat(target_cols // 2, BLK)
    factor_tile = jnp.zeros((tile_rows, col_blocks, BLK), jnp.float32)
    for step_index in range(lax.axis_size("front")):
        first_block = step_index * col_blocks
        panel_slots = first_block + jnp.arange(col_blocks, dtype=jnp.int32)
        sep_cols = front_tile.reshape(tile_rows, 2 * col_blocks, BLK)[:, 0::2].reshape(
            tile_rows, panel_width
        )
        panel_rows = spread(sep_cols, "front", step_index)
        wanted = jnp.concatenate([2 * panel_slots, target_cols])
        fetched = fetch_rows(panel_rows, wanted, level_depth, leaf_index)
        chol_block = jnp.linalg.cholesky(fetched[:panel_width])
        own_factor = solve_rows(chol_block, panel_rows)
        col_factor = solve_rows(chol_block, fetched[panel_width:])
        own_keep = (row_odd | (row_sep >= first_block + col_blocks)).astype(jnp.float32)
        col_keep = (col_odd | (col_sep >= first_block + col_blocks)).astype(jnp.float32)
        front_tile = front_tile - jnp.dot(
            own_factor * own_keep[:, None], (col_factor * col_keep[:, None]).T, precision=HIGHEST
        )
        valid_rows = (row_odd[:, None] | (row_sep[:, None] >= panel_slots[None, :])).astype(
            jnp.float32
        )
        factor_tile = jnp.where(
            front_index == step_index,
            own_factor.reshape(tile_rows, col_blocks, BLK) * valid_rows[:, :, None],
            factor_tile,
        )
    schur_tile = front_tile.reshape(tile_rows // BLK, BLK, 2 * col_blocks, BLK)[
        1::2, :, 1::2, :
    ].reshape(tile_rows // 2, col_blocks * BLK)
    return (factor_tile.reshape(tile_rows, col_blocks * BLK), schur_tile)


def per_device(
    child_updates,
    initial_one,
    initial_two,
    pattern_one,
    pattern_two,
    parent_map_one,
    parent_map_two,
):
    leaf_index = lax.axis_index("leaf")
    front_index = lax.axis_index("front")
    col_blocks = SEP // BLK // lax.axis_size("front")
    child_tile = child_updates
    factors = []
    for level_depth, initial, pattern, parent_map in (
        (1, initial_one, pattern_one, parent_map_one),
        (2, initial_two, pattern_two, parent_map_two),
    ):
        front_tile, row_ids, target_cols = assemble(
            child_tile,
            initial,
            pattern,
            parent_map,
            level_depth,
            leaf_index,
            front_index,
            col_blocks,
        )
        factor_tile, child_tile = factor_panels(
            front_tile, row_ids, target_cols, level_depth, leaf_index, front_index, col_blocks
        )
        factors.append(factor_tile)
    return (factors[0], factors[1], child_tile)


def solution(mesh):
    placed = (P("leaf", "front"), P("leaf", "front"), P("leaf", "front"), P(), P(), P(), P())
    return jax.shard_map(
        per_device,
        mesh=mesh,
        in_specs=placed,
        out_specs=(P("leaf", "front"), P("leaf", "front"), P("leaf", "front")),
        check_vma=False,
    )
```

profile of v0, /device:TPU:1, one launch (start us, length us, event | category | flops | bytes accessed | tf_op | source)
XLA Modules:
  0.0 1970.0 jit_solution(7487446941033398264)
XLA Ops:
  8.1 65.2 %all-gather.3.cloned.1.call-done = f32[1024,1024]{1,0:T(8,128)} async-done(((f32[1024,128]{1,0:T(8,128)}), f32[1024,1024]{1,0:T(8,128)}) %all-gather.3.cloned.1.call-update) | async-done | bytes 4194320 | tf_op jit(solution)/shard_map/all_gather | solution.py:72
  82.8 5.5 collective-permute-start
  96.0 64.8 %all-reduce.17.cloned.1.call-done = f32[1024,128]{0,1:T(8,128)} async-done(((f32[1024,128]{0,1:T(8,128)}), f32[1024,128]{0,1:T(8,128)}) %all-reduce.17.cloned.1.call-update) | async-done | bytes 524304 | tf_op jit(solution)/shard_map/psum | solution.py:25
  172.7 11.7 cholesky.254
  185.8 9.8 custom-call.40
  198.7 67.0 %all-reduce.19.cloned.1.call-done = f32[1024,128]{0,1:T(8,128)} async-done(((f32[1024,128]{0,1:T(8,128)}), f32[1024,128]{0,1:T(8,128)}) %all-reduce.19.cloned.1.call-update) | async-done | bytes 524304 | tf_op jit(solution)/shard_map/psum | solution.py:25
  265.7 5.6 collective-permute-start.2
  277.9 11.7 cholesky.265
  291.0 9.8 custom-call.42
  303.9 67.0 %all-reduce.21.cloned.1.call-done = f32[1024,128]{0,1:T(8,128)} async-done(((f32[1024,128]{0,1:T(8,128)}), f32[1024,128]{0,1:T(8,128)}) %all-reduce.21.cloned.1.call-update) | async-done | bytes 524304 | tf_op jit(solution)/shard_map/psum | solution.py:25
  382.9 11.7 cholesky.276
  395.9 9.8 custom-call.44
  408.9 67.0 %all-reduce.23.cloned.1.call-done = f32[1024,128]{0,1:T(8,128)} async-done(((f32[1024,128]{0,1:T(8,128)}), f32[1024,128]{0,1:T(8,128)}) %all-reduce.23.cloned.1.call-update) | async-done | bytes 524304 | tf_op jit(solution)/shard_map/psum | solution.py:25
  488.0 11.7 cholesky.287
  501.1 9.8 custom-call.46
  513.9 67.0 %all-reduce.25.cloned.1.call-done = f32[1024,128]{0,1:T(8,128)} async-done(((f32[1024,128]{0,1:T(8,128)}), f32[1024,128]{0,1:T(8,128)}) %all-reduce.25.cloned.1.call-update) | async-done | bytes 524304 | tf_op jit(solution)/shard_map/psum | solution.py:25
  581.0 5.5 collective-permute-start.5
  593.1 11.7 cholesky.298
  606.1 9.8 custom-call.48
  619.1 67.0 %all-reduce.27.cloned.1.call-done = f32[1024,128]{0,1:T(8,128)} async-done(((f32[1024,128]{0,1:T(8,128)}), f32[1024,128]{0,1:T(8,128)}) %all-reduce.27.cloned.1.call-update) | async-done | bytes 524304 | tf_op jit(solution)/shard_map/psum | solution.py:25
  686.1 5.7 collective-permute-start.6
  698.4 11.7 cholesky.309
  711.4 9.8 custom-call.50
  724.3 67.1 %all-reduce.29.cloned.1.call-done = f32[1024,128]{0,1:T(8,128)} async-done(((f32[1024,128]{0,1:T(8,128)}), f32[1024,128]{0,1:T(8,128)}) %all-reduce.29.cloned.1.call-update) | async-done | bytes 524304 | tf_op jit(solution)/shard_map/psum | solution.py:25
  803.4 11.7 cholesky.320
  816.4 9.8 custom-call.52
  829.3 67.1 %all-reduce.31.cloned.1.call-done = f32[1024,128]{0,1:T(8,128)} async-done(((f32[1024,128]{0,1:T(8,128)}), f32[1024,128]{0,1:T(8,128)}) %all-reduce.31.cloned.1.call-update) | async-done | bytes 524304 | tf_op jit(solution)/shard_map/psum | solution.py:25
  908.4 11.7 cholesky.331
  921.5 9.8 custom-call.54
  936.3 40.7 %all-gather.5.cloned.1.call-done = f32[512,1024]{1,0:T(8,128)} async-done(((f32[512,128]{1,0:T(8,128)}), f32[512,1024]{1,0:T(8,128)}) %all-gather.5.cloned.1.call-update) | async-done | bytes 2097168 | tf_op jit(solution)/shard_map/all_gather | solution.py:72
  987.9 15.9 collective-permute-done.9
  1005.3 6.0 collective-permute-start.10
  1016.5 65.7 %all-reduce.33.cloned.1.call-done = f32[512,128]{0,1:T(8,128)} async-done(((f32[512,128]{0,1:T(8,128)}), f32[512,128]{0,1:T(8,128)}) %all-reduce.33.cloned.1.call-update) | async-done | bytes 262160 | tf_op jit(solution)/shard_map/psum | solution.py:25
  1091.7 11.8 collective-permute-done.12
  1107.2 11.7 cholesky.342
  1120.2 9.8 custom-call.56
  1132.3 67.0 %all-reduce.35.cloned.1.call-done = f32[512,128]{0,1:T(8,128)} async-done(((f32[512,128]{0,1:T(8,128)}), f32[512,128]{0,1:T(8,128)}) %all-reduce.35.cloned.1.call-update) | async-done | bytes 262160 | tf_op jit(solution)/shard_map/psum | solution.py:25
  1208.6 11.8 collective-permute-done.14
  1224.1 11.7 cholesky.353
  1237.1 9.8 custom-call.58
  1249.3 67.1 %all-reduce.37.cloned.1.call-done = f32[512,128]{0,1:T(8,128)} async-done(((f32[512,128]{0,1:T(8,128)}), f32[512,128]{0,1:T(8,128)}) %all-reduce.37.cloned.1.call-update) | async-done | bytes 262160 | tf_op jit(solution)/shard_map/psum | solution.py:25
  1325.7 11.8 collective-permute-done.16
  1341.2 11.7 cholesky.364
  1354.2 9.8 custom-call.60
  1366.4 67.0 %all-reduce.39.cloned.1.call-done = f32[512,128]{0,1:T(8,128)} async-done(((f32[512,128]{0,1:T(8,128)}), f32[512,128]{0,1:T(8,128)}) %all-reduce.39.cloned.1.call-update) | async-done | bytes 262160 | tf_op jit(solution)/shard_map/psum | solution.py:25
  1442.7 11.8 collective-permute-done.18
  1458.2 11.7 cholesky.375
  1471.3 9.8 custom-call.62
  1483.5 67.0 %all-reduce.41.cloned.1.call-done = f32[512,128]{0,1:T(8,128)} async-done(((f32[512,128]{0,1:T(8,128)}), f32[512,128]{0,1:T(8,128)}) %all-reduce.41.cloned.1.call-update) | async-done | bytes 262160 | tf_op jit(solution)/shard_map/psum | solution.py:25
  1560.0 11.8 collective-permute-done.20
  1575.5 11.7 cholesky.386
  1588.6 9.8 custom-call.64
  1600.8 67.0 %all-reduce.43.cloned.1.call-done = f32[512,128]{0,1:T(8,128)} async-done(((f32[512,128]{0,1:T(8,128)}), f32[512,128]{0,1:T(8,128)}) %all-reduce.43.cloned.1.call-update) | async-done | bytes 262160 | tf_op jit(solution)/shard_map/psum | solution.py:25
  1677.0 11.8 collective-permute-done.22
  1692.5 11.7 cholesky.397
  1705.6 9.8 custom-call.66
  1718.5 67.0 %all-reduce.45.cloned.1.call-done = f32[512,128]{0,1:T(8,128)} async-done(((f32[512,128]{0,1:T(8,128)}), f32[512,128]{0,1:T(8,128)}) %all-reduce.45.cloned.1.call-update) | async-done | bytes 262160 | tf_op jit(solution)/shard_map/psum | solution.py:25
  1795.9 10.7 collective-permute-done.24
  1810.3 11.7 cholesky.408
  1823.4 10.4 custom-call.68
  1840.7 67.0 %all-reduce.47.cloned.1.call-done = f32[512,128]{0,1:T(8,128)} async-done(((f32[512,128]{0,1:T(8,128)}), f32[512,128]{0,1:T(8,128)}) %all-reduce.47.cloned.1.call-update) | async-done | bytes 262160 | tf_op jit(solution)/shard_map/psum | solution.py:25
  1922.2 7.6 collective-permute-done.26
  1935.3 11.7 cholesky.419
  1948.4 9.8 custom-call.70
  (601 shorter events, 299.2 us)
Async XLA Ops:
  7.2 66.1 %all-gather.3.cloned.1.call-start = ((), (), s32[]{:S(2)}) async-start(), calls=%async_computation | async-start | bytes 4718592 | tf_op jit(solution)/shard_map/all_gather | solution.py:72
  7.9 152.8 %all-reduce.17.cloned.1.call-start = ((), (), s32[]{:S(2)}) async-start(), calls=%async_computation.1 | async-start | bytes 1048576 | tf_op jit(solution)/shard_map/psum | solution.py:25
  82.8 10.4 collective-permute-start
  95.8 169.9 %all-reduce.19.cloned.1.call-start = ((), (), s32[]{:S(2)}) async-start(), calls=%async_computation.2 | async-start | bytes 1048576 | tf_op jit(solution)/shard_map/psum | solution.py:25
  95.9 812.2 %copy-start.63 = (pred[3]{0:T(512)(128)(4,1)}, pred[3]{0:T(512)(128)(4,1)S(1)}, u32[]{:S(2)}) copy-start(pred[3]{0:T(512)(128)(4,1)S(1)} %get-tuple-element.14) | copy-start | bytes 13
  160.7 7.2 collective-permute-start.1
  198.6 172.3 %all-reduce.21.cloned.1.call-start = ((), (), s32[]{:S(2)}) async-start(), calls=%async_computation.3 | async-start | bytes 1048576 | tf_op jit(solution)/shard_map/psum | solution.py:25
  265.7 7.4 collective-permute-start.2
  303.8 172.1 %all-reduce.23.cloned.1.call-start = ((), (), s32[]{:S(2)}) async-start(), calls=%async_computation.4 | async-start | bytes 1048576 | tf_op jit(solution)/shard_map/psum | solution.py:25
  303.9 602.3 %copy-start.62 = (s32[1024]{0:T(1024)}, s32[1024]{0:T(1024)S(1)}, u32[]{:S(2)}) copy-start(s32[1024]{0:T(1024)S(1)} %get-tuple-element.48) | copy-start | bytes 12292
  370.9 7.1 collective-permute-start.3
  408.7 172.2 %all-reduce.25.cloned.1.call-start = ((), (), s32[]{:S(2)}) async-start(), calls=%async_computation.5 | async-start | bytes 1048576 | tf_op jit(solution)/shard_map/psum | solution.py:25
  475.9 7.2 collective-permute-start.4
  513.9 172.2 %all-reduce.27.cloned.1.call-start = ((), (), s32[]{:S(2)}) async-start(), calls=%async_computation.6 | async-start | bytes 1048576 | tf_op jit(solution)/shard_map/psum | solution.py:25
  581.0 7.2 collective-permute-start.5
  586.6 30.4 %copy-start.43 = (f32[1024]{0:T(1024)}, f32[1024]{0:T(1024)S(1)}, u32[]{:S(2)}) copy-start(f32[1024]{0:T(1024)S(1)} %broadcast_bitcast_fusion.4) | copy-start | bytes 12292
  619.0 172.4 %all-reduce.29.cloned.1.call-start = ((), (), s32[]{:S(2)}) async-start(), calls=%async_computation.7 | async-start | bytes 1048576 | tf_op jit(solution)/shard_map/psum | solution.py:25
  686.1 7.4 collective-permute-start.6
  691.9 30.4 %copy-start.45 = (f32[1024]{0:T(1024)}, f32[1024]{0:T(1024)S(1)}, u32[]{:S(2)}) copy-start(f32[1024]{0:T(1024)S(1)} %broadcast_bitcast_fusion.3) | copy-start | bytes 12292
  724.2 172.1 %all-reduce.31.cloned.1.call-start = ((), (), s32[]{:S(2)}) async-start(), calls=%async_computation.8 | async-start | bytes 1048576 | tf_op jit(solution)/shard_map/psum | solution.py:25
  791.4 7.1 collective-permute-start.7
  796.9 30.4 %copy-start.47 = (f32[1024]{0:T(1024)}, f32[1024]{0:T(1024)S(1)}, u32[]{:S(2)}) copy-start(f32[1024]{0:T(1024)S(1)} %broadcast_bitcast_fusion.2) | copy-start | bytes 12292
  829.2 147.8 %all-gather.5.cloned.1.call-start = ((), (), s32[]{:S(2)}) async-start(), calls=%async_computation.9 | async-start | bytes 2359296 | tf_op jit(solution)/shard_map/all_gather | solution.py:72
  896.4 7.2 collective-permute-start.8
  935.2 147.0 %all-reduce.33.cloned.1.call-start = ((), (), s32[]{:S(2)}) async-start(), calls=%async_computation.10 | async-start | bytes 524288 | tf_op jit(solution)/shard_map/psum | solution.py:25
  983.8 20.0 %collective-permute-start.9 = (f32[1024,256]{0,1:T(8,128)}, f32[1024,256]{0,1:T(8,128)}, u32[]{:S(2)}, u32[]{:S(2)}) collective-permute-start(f32[1024,256]{0,1:T(8,128)} %copy.86), channel_id=1, source_target_pairs={{0,16},{16,0},{8,24},{24,8},{32,48},{48,32},{40,56},{56,40},{64,80... | collective-permute-start | bytes 3145736 | tf_op jit(solution)/shard_map/ppermute | solution.py:20
  1005.3 9.0 collective-permute-start.10
  1016.5 182.9 %all-reduce.35.cloned.1.call-start = ((), (), s32[]{:S(2)}) async-start(), calls=%async_computation.11 | async-start | bytes 524288 | tf_op jit(solution)/shard_map/psum | solution.py:25
  1082.2 6.6 collective-permute-start.11
  1089.8 13.7 collective-permute-start.12
  1091.7 39.2 %copy-start.49 = (f32[512]{0:T(512)}, f32[512]{0:T(512)S(1)}, u32[]{:S(2)}) copy-start(f32[512]{0:T(512)S(1)} %broadcast_bitcast_fusion.17) | copy-start | bytes 6148
  1132.3 184.1 %all-reduce.37.cloned.1.call-start = ((), (), s32[]{:S(2)}) async-start(), calls=%async_computation.12 | async-start | bytes 524288 | tf_op jit(solution)/shard_map/psum | solution.py:25
  1199.4 6.6 collective-permute-start.13
  1207.0 13.4 collective-permute-start.14
  1208.6 39.2 %copy-start.51 = (f32[512]{0:T(512)}, f32[512]{0:T(512)S(1)}, u32[]{:S(2)}) copy-start(f32[512]{0:T(512)S(1)} %broadcast_bitcast_fusion.16) | copy-start | bytes 6148
  1249.3 184.1 %all-reduce.39.cloned.1.call-start = ((), (), s32[]{:S(2)}) async-start(), calls=%async_computation.13 | async-start | bytes 524288 | tf_op jit(solution)/shard_map/psum | solution.py:25
  1316.4 6.6 collective-permute-start.15
  1324.1 13.4 collective-permute-start.16
  1325.7 39.2 %copy-start.53 = (f32[512]{0:T(512)}, f32[512]{0:T(512)S(1)}, u32[]{:S(2)}) copy-start(f32[512]{0:T(512)S(1)} %broadcast_bitcast_fusion.15) | copy-start | bytes 6148
  1366.4 184.1 %all-reduce.41.cloned.1.call-start = ((), (), s32[]{:S(2)}) async-start(), calls=%async_computation.14 | async-start | bytes 524288 | tf_op jit(solution)/shard_map/psum | solution.py:25
  1433.4 6.6 collective-permute-start.17
  1441.1 13.5 collective-permute-start.18
  1442.7 39.2 %copy-start.55 = (f32[512]{0:T(512)}, f32[512]{0:T(512)S(1)}, u32[]{:S(2)}) copy-start(f32[512]{0:T(512)S(1)} %broadcast_bitcast_fusion.14) | copy-start | bytes 6148
  1483.4 184.4 %all-reduce.43.cloned.1.call-start = ((), (), s32[]{:S(2)}) async-start(), calls=%async_computation.15 | async-start | bytes 524288 | tf_op jit(solution)/shard_map/psum | solution.py:25
  1550.5 6.6 collective-permute-start.19
  1558.2 13.7 collective-permute-start.20
  1560.0 39.3 %copy-start.57 = (f32[512]{0:T(512)}, f32[512]{0:T(512)S(1)}, u32[]{:S(2)}) copy-start(f32[512]{0:T(512)S(1)} %broadcast_bitcast_fusion.13) | copy-start | bytes 6148
  1600.7 184.8 %all-reduce.45.cloned.1.call-start = ((), (), s32[]{:S(2)}) async-start(), calls=%async_computation.16 | async-start | bytes 524288 | tf_op jit(solution)/shard_map/psum | solution.py:25
  1667.8 6.6 collective-permute-start.21
  1675.5 13.4 collective-permute-start.22
  1677.0 39.2 %copy-start.59 = (f32[512]{0:T(512)}, f32[512]{0:T(512)S(1)}, u32[]{:S(2)}) copy-start(f32[512]{0:T(512)S(1)} %broadcast_bitcast_fusion.12) | copy-start | bytes 6148
  1716.2 90.6 %copy-start.23 = (f32[128,512]{1,0:T(8,128)}, f32[128,512]{1,0:T(8,128)S(1)}, u32[]{:S(2)}) copy-start(f32[128,512]{1,0:T(8,128)S(1)} %fusion.49) | copy-start | bytes 786436
  1718.4 189.3 %all-reduce.47.cloned.1.call-start = ((), (), s32[]{:S(2)}) async-start(), calls=%async_computation.17 | async-start | bytes 524288 | tf_op jit(solution)/shard_map/psum | solution.py:25
  1785.5 6.6 collective-permute-start.23
  1793.2 13.4 collective-permute-start.24
  1833.9 83.7 %copy-start.3 = (f32[128,1024]{1,0:T(8,128)S(1)}, f32[128,1024]{1,0:T(8,128)}, u32[]{:S(2)}) copy-start(f32[128,1024]{1,0:T(8,128)} %copy-done.2) | copy-start | bytes 1572868
  1833.9 83.7 %copy-start.5 = (f32[128,1024]{1,0:T(8,128)S(1)}, f32[128,1024]{1,0:T(8,128)}, u32[]{:S(2)}) copy-start(f32[128,1024]{1,0:T(8,128)} %copy-done.4) | copy-start | bytes 1572868
  1833.9 83.7 %copy-start.7 = (f32[128,1024]{1,0:T(8,128)S(1)}, f32[128,1024]{1,0:T(8,128)}, u32[]{:S(2)}) copy-start(f32[128,1024]{1,0:T(8,128)} %copy-done.6) | copy-start | bytes 1572868
  1833.9 83.7 %copy-start.9 = (f32[128,1024]{1,0:T(8,128)S(1)}, f32[128,1024]{1,0:T(8,128)}, u32[]{:S(2)}) copy-start(f32[128,1024]{1,0:T(8,128)} %copy-done.8) | copy-start | bytes 1572868
  1835.3 82.4 %copy-start.44 = (f32[1024]{0:T(1024)S(1)}, f32[1024]{0:T(1024)}, u32[]{:S(2)}) copy-start(f32[1024]{0:T(1024)} %copy-done.43) | copy-start | bytes 12292
  1835.3 82.4 %copy-start.46 = (f32[1024]{0:T(1024)S(1)}, f32[1024]{0:T(1024)}, u32[]{:S(2)}) copy-start(f32[1024]{0:T(1024)} %copy-done.45) | copy-start | bytes 12292
  1835.3 82.4 %copy-start.48 = (f32[1024]{0:T(1024)S(1)}, f32[1024]{0:T(1024)}, u32[]{:S(2)}) copy-start(f32[1024]{0:T(1024)} %copy-done.47) | copy-start | bytes 12292
  1907.7 6.6 collective-permute-start.25
  1916.1 13.7 collective-permute-start.26
  (49 other events, 881.8 us)
Sparse Core Ops, SparseCore 0:
  9.7 63.4 all-gather.2
  95.9 64.7 all-reduce.16
  198.7 66.9 all-reduce.18
  303.9 66.9 all-reduce.20
  408.9 67.0 all-reduce.22
  514.0 66.9 all-reduce.24
  619.1 66.9 all-reduce.26
  724.3 66.9 all-reduce.28
  829.3 66.9 all-reduce.30
  935.3 41.6 all-gather.4
  1016.6 65.5 all-reduce.32
  1132.4 66.9 all-reduce.34
  1249.4 66.9 all-reduce.36
  1366.5 66.9 all-reduce.38
  1483.5 66.9 all-reduce.40
  1600.8 66.9 all-reduce.42
  1718.6 66.9 all-reduce.44
  1840.7 66.9 all-reduce.46
where the time goes:
time: 1980 us; the launch traced here: 1970 us
  waiting for transfers between devices  1300 us (66%)
  other arithmetic  415 us (21%)
  starting transfers between devices  111 us (6%)
  local copies, waits for them, and re-layouts  86 us (4%)
  matrix products  35.7 us (2%)
    psum x16, waiting for transfers between devices, spread(): return lax.psum(block, axis)  1070 us
    another operation x48, other arithmetic, factor_panels(): chol_block = jnp.linalg.cholesky(fetched[:panel_width])  198 us
    another operation x32, other arithmetic, solve_rows(): jax.scipy.linalg.solve_triangular(chol_block, right_side.T, lower=True)  168 us
    ppermute x27, waiting for transfers between devices, swapped(): return lax.ppermute(block, axis, route)  128 us
    ppermute x27, starting transfers between devices, swapped(): return lax.ppermute(block, axis, route)  110 us
    all_gather x2, waiting for transfers between devices, assemble(): gathered = lax.all_gather(child_tile, 'front', axis=1, tiled=True)  106 us
  transfers between devices with their start and end apart: 45, of which 43 were waited for; matrix products, arithmetic and copies ran while one was open for 1% of the time, Pallas kernels for 0%

commit v1 on v0

--- a/solution.py
+++ b/solution.py
@@ -69,7 +69,14 @@
     update_blocks = UPD // BLK
     front_blocks = FR // BLK
     tile_cols = 2 * col_blocks * BLK
-    gathered = lax.all_gather(child_tile, "front", axis=1, tiled=True)
+    ring = [child_tile]
+    for hop in range(7):
+        ring.append(lax.ppermute(ring[-1], "front", [(dev, (dev + 1) % 8) for dev in range(8)]))
+    gathered = jnp.roll(
+        jnp.concatenate(ring[::-1], axis=1),
+        (lax.axis_index("front") + 1) * ring[0].shape[1],
+        axis=1,
+    )
     child_rows = gathered.shape[0]
     child_row_blocks = child_rows // BLK
     both_maps = lax.dynamic_index_in_dim(parent_map, front_group, 0, keepdims=False)

time: 1980 us -> 2040 us (1.030)
  waiting for transfers between devices: 1300 us -> 1330 us
    ppermute x0 -> x14, waiting for transfers between devices: none -> 134 us  [assemble(): lax.ppermute(ring[-1], 'front', [(dev, (dev + 1) % 8) for dev in range(8)])]
    all_gather x2 -> x0, waiting for transfers between devices: 106 us -> none  [assemble(): gathered = lax.all_gather(child_tile, 'front', axis=1, tiled=True)]
  transfers between devices with their start and end apart: 45 -> 57, of which waited for: 43 -> 55; matrix products, arithmetic and copies ran while one was open for 1% -> 1% of each run, Pallas kernels for 0% -> 0%
where the time goes in v1:
time: 2040 us; the launch traced here: 2030 us
  waiting for transfers between devices  1330 us (65%)
  other arithmetic  423 us (21%)
  starting transfers between devices  119 us (6%)
  local copies, waits for them, and re-layouts  96.3 us (5%)
  matrix products  41.8 us (2%)
    psum x16, waiting for transfers between devices, spread(): return lax.psum(block, axis)  1070 us
    another operation x48, other arithmetic, factor_panels(): chol_block = jnp.linalg.cholesky(fetched[:panel_width])  201 us
    another operation x32, other arithmetic, solve_rows(): jax.scipy.linalg.solve_triangular(chol_block, right_side.T, lower=True)  170 us
    ppermute x14, waiting for transfers between devices, assemble(): lax.ppermute(ring[-1], 'front', [(dev, (dev + 1) % 8) for dev in range(8)])  134 us
    ppermute x27, waiting for transfers between devices, swapped(): return lax.ppermute(block, axis, route)  125 us
    ppermute x27, starting transfers between devices, swapped(): return lax.ppermute(block, axis, route)  115 us
  transfers between devices with their start and end apart: 57, of which 55 were waited for; matrix products, arithmetic and copies ran while one was open for 1% of the time, Pallas kernels for 0%

profile of v1, /device:TPU:1, one launch (start us, length us, event | category | flops | bytes accessed | tf_op | source)
XLA Modules:
  0.0 2029.3 jit_solution(15408159403474425599)
XLA Ops:
  9.8 15.8 collective-permute-done
  25.6 13.4 collective-permute-done.1
  39.0 12.5 collective-permute-done.2
  51.5 11.6 collective-permute-done.3
  63.0 10.6 collective-permute-done.4
  74.4 9.8 collective-permute-done.5
  84.7 10.4 collective-permute-done.6
  124.0 67.2 %all-reduce.17.cloned.1.call-done = f32[1024,128]{0,1:T(8,128)} async-done(((f32[1024,128]{0,1:T(8,128)}), f32[1024,128]{0,1:T(8,128)}) %all-reduce.17.cloned.1.call-update) | async-done | bytes 524304 | tf_op jit(solution)/shard_map/psum | solution.py:25
  203.4 11.7 cholesky.254
  216.5 9.8 custom-call.40
  229.4 67.0 %all-reduce.19.cloned.1.call-done = f32[1024,128]{0,1:T(8,128)} async-done(((f32[1024,128]{0,1:T(8,128)}), f32[1024,128]{0,1:T(8,128)}) %all-reduce.19.cloned.1.call-update) | async-done | bytes 524304 | tf_op jit(solution)/shard_map/psum | solution.py:25
  308.4 11.7 cholesky.265
  321.4 9.8 custom-call.42
  334.3 67.1 %all-reduce.21.cloned.1.call-done = f32[1024,128]{0,1:T(8,128)} async-done(((f32[1024,128]{0,1:T(8,128)}), f32[1024,128]{0,1:T(8,128)}) %all-reduce.21.cloned.1.call-update) | async-done | bytes 524304 | tf_op jit(solution)/shard_map/psum | solution.py:25
  413.4 11.7 cholesky.276
  426.4 9.8 custom-call.44
  439.4 66.9 %all-reduce.23.cloned.1.call-done = f32[1024,128]{0,1:T(8,128)} async-done(((f32[1024,128]{0,1:T(8,128)}), f32[1024,128]{0,1:T(8,128)}) %all-reduce.23.cloned.1.call-update) | async-done | bytes 524304 | tf_op jit(solution)/shard_map/psum | solution.py:25
  518.3 11.7 cholesky.287
  531.4 9.8 custom-call.46
  545.2 67.0 %all-reduce.25.cloned.1.call-done = f32[1024,128]{0,1:T(8,128)} async-done(((f32[1024,128]{0,1:T(8,128)}), f32[1024,128]{0,1:T(8,128)}) %all-reduce.25.cloned.1.call-update) | async-done | bytes 524304 | tf_op jit(solution)/shard_map/psum | solution.py:25
  624.5 11.7 cholesky.298
  637.6 9.8 custom-call.48
  651.5 67.1 %all-reduce.27.cloned.1.call-done = f32[1024,128]{0,1:T(8,128)} async-done(((f32[1024,128]{0,1:T(8,128)}), f32[1024,128]{0,1:T(8,128)}) %all-reduce.27.cloned.1.call-update) | async-done | bytes 524304 | tf_op jit(solution)/shard_map/psum | solution.py:25
  730.5 11.7 cholesky.309
  743.5 9.8 custom-call.50
  757.4 67.1 %all-reduce.29.cloned.1.call-done = f32[1024,128]{0,1:T(8,128)} async-done(((f32[1024,128]{0,1:T(8,128)}), f32[1024,128]{0,1:T(8,128)}) %all-reduce.29.cloned.1.call-update) | async-done | bytes 524304 | tf_op jit(solution)/shard_map/psum | solution.py:25
  836.5 11.7 cholesky.320
  849.6 9.8 custom-call.52
  863.5 67.0 %all-reduce.31.cloned.1.call-done = f32[1024,128]{0,1:T(8,128)} async-done(((f32[1024,128]{0,1:T(8,128)}), f32[1024,128]{0,1:T(8,128)}) %all-reduce.31.cloned.1.call-update) | async-done | bytes 524304 | tf_op jit(solution)/shard_map/psum | solution.py:25
  942.7 11.7 cholesky.331
  955.8 9.8 custom-call.54
  1032.5 13.3 collective-permute-done.23
  1047.2 8.6 collective-permute-start.24
  1061.1 65.9 %all-reduce.33.cloned.1.call-done = f32[512,128]{0,1:T(8,128)} async-done(((f32[512,128]{0,1:T(8,128)}), f32[512,128]{0,1:T(8,128)}) %all-reduce.33.cloned.1.call-update) | async-done | bytes 262160 | tf_op jit(solution)/shard_map/psum | solution.py:25
  1136.3 11.8 collective-permute-done.26
  1151.8 11.7 cholesky.342
  1164.9 9.8 custom-call.56
  1177.0 67.0 %all-reduce.35.cloned.1.call-done = f32[512,128]{0,1:T(8,128)} async-done(((f32[512,128]{0,1:T(8,128)}), f32[512,128]{0,1:T(8,128)}) %all-reduce.35.cloned.1.call-update) | async-done | bytes 262160 | tf_op jit(solution)/shard_map/psum | solution.py:25
  1253.4 11.8 collective-permute-done.28
  1269.0 11.7 cholesky.353
  1282.0 9.8 custom-call.58
  1294.2 67.0 %all-reduce.37.cloned.1.call-done = f32[512,128]{0,1:T(8,128)} async-done(((f32[512,128]{0,1:T(8,128)}), f32[512,128]{0,1:T(8,128)}) %all-reduce.37.cloned.1.call-update) | async-done | bytes 262160 | tf_op jit(solution)/shard_map/psum | solution.py:25
  1370.4 11.8 collective-permute-done.30
  1386.0 11.7 cholesky.364
  1399.0 9.8 custom-call.60
  1411.2 67.0 %all-reduce.39.cloned.1.call-done = f32[512,128]{0,1:T(8,128)} async-done(((f32[512,128]{0,1:T(8,128)}), f32[512,128]{0,1:T(8,128)}) %all-reduce.39.cloned.1.call-update) | async-done | bytes 262160 | tf_op jit(solution)/shard_map/psum | solution.py:25
  1487.5 11.8 collective-permute-done.32
  1503.0 11.7 cholesky.375
  1516.1 9.8 custom-call.62
  1528.2 67.0 %all-reduce.41.cloned.1.call-done = f32[512,128]{0,1:T(8,128)} async-done(((f32[512,128]{0,1:T(8,128)}), f32[512,128]{0,1:T(8,128)}) %all-reduce.41.cloned.1.call-update) | async-done | bytes 262160 | tf_op jit(solution)/shard_map/psum | solution.py:25
  1604.6 11.8 collective-permute-done.34
  1620.1 11.7 cholesky.386
  1633.1 9.8 custom-call.64
  1645.3 67.0 %all-reduce.43.cloned.1.call-done = f32[512,128]{0,1:T(8,128)} async-done(((f32[512,128]{0,1:T(8,128)}), f32[512,128]{0,1:T(8,128)}) %all-reduce.43.cloned.1.call-update) | async-done | bytes 262160 | tf_op jit(solution)/shard_map/psum | solution.py:25
  1721.8 11.8 collective-permute-done.36
  1737.3 11.7 cholesky.397
  1750.4 9.8 custom-call.66
  1763.3 67.1 %all-reduce.45.cloned.1.call-done = f32[512,128]{0,1:T(8,128)} async-done(((f32[512,128]{0,1:T(8,128)}), f32[512,128]{0,1:T(8,128)}) %all-reduce.45.cloned.1.call-update) | async-done | bytes 262160 | tf_op jit(solution)/shard_map/psum | solution.py:25
  1840.8 10.7 collective-permute-done.38
  1864.3 13.2 cholesky.408
  1881.1 11.3 custom-call.68
  1899.8 67.0 %all-reduce.47.cloned.1.call-done = f32[512,128]{0,1:T(8,128)} async-done(((f32[512,128]{0,1:T(8,128)}), f32[512,128]{0,1:T(8,128)}) %all-reduce.47.cloned.1.call-update) | async-done | bytes 262160 | tf_op jit(solution)/shard_map/psum | solution.py:25
  1994.2 11.7 cholesky.419
  2007.3 9.8 custom-call.70
  (653 shorter events, 405.6 us)
Async XLA Ops:
  7.2 91.6 %copy-start.30 = (f32[1024,128]{1,0:T(8,128)S(1)}, f32[1024,128]{1,0:T(8,128)}, u32[]{:S(2)}) copy-start(f32[1024,128]{1,0:T(8,128)} %param.16) | copy-start | bytes 1572868
  7.2 184.0 %all-reduce.17.cloned.1.call-start = ((), (), s32[]{:S(2)}) async-start(), calls=%async_computation | async-start | bytes 1048576 | tf_op jit(solution)/shard_map/psum | solution.py:25
  7.2 18.3 collective-permute-start
  25.6 13.4 collective-permute-start.1
  39.0 12.5 collective-permute-start.2
  51.5 11.6 collective-permute-start.3
  63.0 10.6 collective-permute-start.4
  74.4 9.8 collective-permute-start.5
  84.3 10.8 collective-permute-start.6
  109.4 11.8 collective-permute-start.7
  123.8 172.6 %all-reduce.19.cloned.1.call-start = ((), (), s32[]{:S(2)}) async-start(), calls=%async_computation.1 | async-start | bytes 1048576 | tf_op jit(solution)/shard_map/psum | solution.py:25
  124.0 818.5 %copy-start.61 = (pred[3]{0:T(512)(128)(4,1)}, pred[3]{0:T(512)(128)(4,1)S(1)}, u32[]{:S(2)}) copy-start(pred[3]{0:T(512)(128)(4,1)S(1)} %get-tuple-element.14) | copy-start | bytes 13
  191.2 7.5 collective-permute-start.8
  229.3 172.1 %all-reduce.21.cloned.1.call-start = ((), (), s32[]{:S(2)}) async-start(), calls=%async_computation.2 | async-start | bytes 1048576 | tf_op jit(solution)/shard_map/psum | solution.py:25
  296.4 7.1 collective-permute-start.9
  334.2 172.1 %all-reduce.23.cloned.1.call-start = ((), (), s32[]{:S(2)}) async-start(), calls=%async_computation.3 | async-start | bytes 1048576 | tf_op jit(solution)/shard_map/psum | solution.py:25
  334.3 606.3 %copy-start.60 = (s32[1024]{0:T(1024)}, s32[1024]{0:T(1024)S(1)}, u32[]{:S(2)}) copy-start(s32[1024]{0:T(1024)S(1)} %get-tuple-element.48) | copy-start | bytes 12292
  401.4 7.2 collective-permute-start.10
  439.2 173.1 %all-reduce.25.cloned.1.call-start = ((), (), s32[]{:S(2)}) async-start(), calls=%async_computation.4 | async-start | bytes 1048576 | tf_op jit(solution)/shard_map/psum | solution.py:25
  506.3 7.2 collective-permute-start.11
  545.2 173.4 %all-reduce.27.cloned.1.call-start = ((), (), s32[]{:S(2)}) async-start(), calls=%async_computation.5 | async-start | bytes 1048576 | tf_op jit(solution)/shard_map/psum | solution.py:25
  612.2 7.4 collective-permute-start.12
  651.4 173.1 %all-reduce.29.cloned.1.call-start = ((), (), s32[]{:S(2)}) async-start(), calls=%async_computation.6 | async-start | bytes 1048576 | tf_op jit(solution)/shard_map/psum | solution.py:25
  718.5 7.1 collective-permute-start.13
  757.4 173.2 %all-reduce.31.cloned.1.call-start = ((), (), s32[]{:S(2)}) async-start(), calls=%async_computation.7 | async-start | bytes 1048576 | tf_op jit(solution)/shard_map/psum | solution.py:25
  824.5 7.2 collective-permute-start.14
  863.4 263.6 %all-reduce.33.cloned.1.call-start = ((), (), s32[]{:S(2)}) async-start(), calls=%async_computation.8 | async-start | bytes 524288 | tf_op jit(solution)/shard_map/psum | solution.py:25
  930.5 7.4 collective-permute-start.15
  969.8 8.8 collective-permute-start.16
  978.6 7.8 collective-permute-start.17
  986.4 6.9 collective-permute-start.18
  993.3 6.4 collective-permute-start.19
  999.8 6.6 collective-permute-start.20
  1006.3 7.5 collective-permute-start.21
  1013.8 8.5 collective-permute-start.22
  1028.4 17.4 collective-permute-start.23
  1047.2 11.7 collective-permute-start.24
  1061.1 182.9 %all-reduce.35.cloned.1.call-start = ((), (), s32[]{:S(2)}) async-start(), calls=%async_computation.9 | async-start | bytes 524288 | tf_op jit(solution)/shard_map/psum | solution.py:25
  1127.0 6.6 collective-permute-start.25
  1134.7 13.4 collective-permute-start.26
  1176.9 184.3 %all-reduce.37.cloned.1.call-start = ((), (), s32[]{:S(2)}) async-start(), calls=%async_computation.10 | async-start | bytes 524288 | tf_op jit(solution)/shard_map/psum | solution.py:25
  1244.0 6.6 collective-permute-start.27
  1251.7 13.6 collective-permute-start.28
  1294.1 184.1 %all-reduce.39.cloned.1.call-start = ((), (), s32[]{:S(2)}) async-start(), calls=%async_computation.11 | async-start | bytes 524288 | tf_op jit(solution)/shard_map/psum | solution.py:25
  1361.2 6.6 collective-permute-start.29
  1368.9 13.4 collective-permute-start.30
  1411.2 184.1 %all-reduce.41.cloned.1.call-start = ((), (), s32[]{:S(2)}) async-start(), calls=%async_computation.12 | async-start | bytes 524288 | tf_op jit(solution)/shard_map/psum | solution.py:25
  1478.2 6.6 collective-permute-start.31
  1485.9 13.4 collective-permute-start.32
  1528.2 184.1 %all-reduce.43.cloned.1.call-start = ((), (), s32[]{:S(2)}) async-start(), calls=%async_computation.13 | async-start | bytes 524288 | tf_op jit(solution)/shard_map/psum | solution.py:25
  1595.3 6.6 collective-permute-start.33
  1602.9 13.5 collective-permute-start.34
  1645.3 185.1 %all-reduce.45.cloned.1.call-start = ((), (), s32[]{:S(2)}) async-start(), calls=%async_computation.14 | async-start | bytes 524288 | tf_op jit(solution)/shard_map/psum | solution.py:25
  1712.3 6.6 collective-permute-start.35
  1720.0 13.7 collective-permute-start.36
  1763.2 203.6 %all-reduce.47.cloned.1.call-start = ((), (), s32[]{:S(2)}) async-start(), calls=%async_computation.15 | async-start | bytes 524288 | tf_op jit(solution)/shard_map/psum | solution.py:25
  1830.4 6.6 collective-permute-start.37
  1838.0 13.4 collective-permute-start.38
  1852.6 124.2 %copy-start.3 = (f32[128,1024]{1,0:T(8,128)S(1)}, f32[128,1024]{1,0:T(8,128)}, u32[]{:S(2)}) copy-start(f32[128,1024]{1,0:T(8,128)} %copy-done.2) | copy-start | bytes 1572868
  1852.6 124.2 %copy-start.5 = (f32[128,1024]{1,0:T(8,128)S(1)}, f32[128,1024]{1,0:T(8,128)}, u32[]{:S(2)}) copy-start(f32[128,1024]{1,0:T(8,128)} %copy-done.4) | copy-start | bytes 1572868
  1852.6 124.2 %copy-start.7 = (f32[128,1024]{1,0:T(8,128)S(1)}, f32[128,1024]{1,0:T(8,128)}, u32[]{:S(2)}) copy-start(f32[128,1024]{1,0:T(8,128)} %copy-done.6) | copy-start | bytes 1572868
  1852.6 124.2 %copy-start.9 = (f32[128,1024]{1,0:T(8,128)S(1)}, f32[128,1024]{1,0:T(8,128)}, u32[]{:S(2)}) copy-start(f32[128,1024]{1,0:T(8,128)} %copy-done.8) | copy-start | bytes 1572868
  1966.8 6.6 collective-permute-start.39
  1975.3 13.6 collective-permute-start.40
  (59 other events, 1802.5 us)
Sparse Core Ops, SparseCore 0:
  123.9 67.1 all-reduce.16
  229.4 66.9 all-reduce.18
  334.3 67.0 all-reduce.20
  439.3 66.9 all-reduce.22
  545.3 66.9 all-reduce.24
  651.5 66.9 all-reduce.26
  757.5 66.9 all-reduce.28
  863.6 66.9 all-reduce.30
  1061.2 65.8 all-reduce.32
  1177.0 66.9 all-reduce.34
  1294.3 66.9 all-reduce.36
  1411.3 66.9 all-reduce.38
  1528.3 66.9 all-reduce.40
  1645.4 66.8 all-reduce.42
  1763.4 66.9 all-reduce.44
  1899.9 66.9 all-reduce.46
